TPU v7x, 128 devices: a whole 4x4x4 slice. The times are simulated.
128 devices in a mesh: row: 8 (over y, core), col: 16 (over z, x).
Axes of the slice: x: 4, y: 4, z: 4, core: 2. Of those that a mesh axis runs over, the one named last changes fastest.
Arguments:
- features: bfloat16 [16, 2097152], P(None, ('row', 'col')), may hold values from -6 to 6
- point_weights: bfloat16 [8, 2097152], P(None, ('row', 'col')), may hold values from 0.049804688 to 1
- point_corner: int32 [2097152], P(('row', 'col')), may hold values from 0 to 342
- block_owner: int32 [16384, 1], P(('row', 'col')), may hold values from 0 to 127; in each aligned block of 128 rows (0 to 127, 128 to 255, ...) at most 2 rows name the same one
- block_cell: int32 [16384], P(('row', 'col')), may hold values from 0 to 255
- spec_weight: bfloat16 [64, 64, 16, 16, 128], P('col', 'row'), may hold values from -12 to 12
- skip_weight: bfloat16 [16, 16], replicated, may hold values from -1.5 to 1.5
- mlp_in: bfloat16 [64, 16], replicated, may hold values from -1.5 to 1.5
- mlp_bias: float32 [64], replicated, may hold values from -4 to 4
- mlp_out: bfloat16 [16, 64], replicated, may hold values from -0.75 to 0.75
Outputs:
- point_values: bfloat16 [16, 2097152], P(None, ('row', 'col'))
Inputs may be any that keep to these rules, and one draw needn't show every extreme that they name: `block_owner`: in each aligned block of 128 rows (the point blocks of one device) no device number appears more than 2 times; devices are numbered r * 16 + s over row r and column s.
All inputs are finite; a program needn't handle non-finite values.
Results may differ from a plain program's by a relative error of at most 0.013.
Values may be sent and summed in bfloat16 or wider, within the bound.
No kernel may reach another device: no remote copies, remote signals or barrier semaphores. Data moves between devices by JAX's collectives and lax.ppermute only.
A program may use at most 128 MiB of HBM per device.

v0:
```python
import math
from functools import partial

import jax
import jax.numpy as jnp
import numpy as np
from jax import lax
from jax.experimental import pallas as pl
from jax.experimental.pallas import tpu as pltpu
from jax.sharding import PartitionSpec as P

GRID = 256
MODES = 64
NPTS = 128
NBLK = 128
NSLOT = 256
ROWS = 8
COLS = 16
CH = 16
HID = 64
F32 = jnp.float32
BF16 = jnp.bfloat16
NN = (((1,), (0,)), ((), ()))
NT = (((1,), (1,)), ((), ()))
TN = (((0,), (0,)), ((), ()))


def mm(a, b, dims=NN):
    return lax.dot_general(a, b, dims, preferred_element_type=F32)


ROW_IN = np.array([2 * lo + hi for hi in range(2) for lo in range(8)])
ROW_OUT = np.array([2 * ((-t) % 8) + v for v in range(2) for t in range(8)])


def _freqs():
    j = np.arange(MODES)
    return np.where(j < MODES // 2, j, GRID - MODES + j)


def _trig(freq):
    turns = (np.arange(GRID)[:, None] * freq[None, :]) % GRID
    theta = (2.0 * math.pi / GRID) * turns
    f = 1.0 / math.sqrt(GRID)
    return np.cos(theta) * f, np.sin(theta) * f


def tables():
    cz, sz = _trig(np.arange(MODES))
    cf, sf = _trig(_freqs())
    tz = np.stack([cz, -sz], -1).reshape(GRID, 2 * MODES).T
    fwd = np.stack([np.stack([cf, -sf], -1), np.stack([sf, cf], -1)], 1)
    inv = np.stack(
        [np.stack([cf.T, sf.T], -1), np.stack([-sf.T, cf.T], -1)], 1
    )
    ty = fwd.reshape(COLS, 16, 2, 4, 16, 2)[:, :, :, :, ROW_IN]
    ty = ty.transpose(3, 5, 4, 0, 2, 1).reshape(128, 512)
    tx = fwd.reshape(ROWS, 2, 16, 2, MODES, 2)[:, :, ROW_OUT]
    tx = tx.transpose(5, 4, 0, 1, 3, 2).reshape(128, 512)
    ix = inv.reshape(MODES, 2, ROWS, 2, 16, 2)[:, :, :, :, ROW_IN]
    ix = ix.transpose(2, 3, 5, 4, 1, 0).reshape(512, 128)
    iy = inv.reshape(4, 16, 2, COLS, 16, 2)[:, ROW_OUT]
    iy = iy.transpose(3, 5, 4, 0, 2, 1).reshape(512, 128)
    a = np.where(np.arange(MODES) == 0, 1.0, 2.0)[None, :]
    iz = np.stack([a * cz, -a * sz], -1).reshape(GRID, 2 * MODES)
    return [jnp.asarray(t.astype(np.float32)).astype(BF16) for t in (tz, ty, tx, ix, iy, iz)]


def div_const(v, d):
    return ((v.astype(F32) + 0.5) * (1.0 / d)).astype(jnp.int32)


def pack_kernel(
    row_ref, own_ref, cell_ref, feat_ref, w_ref, corner_ref, mode_hbm,
    send_ref, slot_ref, m1_ref, m2_ref, m3_ref, cnt_ref, head_ref, sem
):
    chip = row_ref[0] // 2
    copies = [
        pltpu.make_async_copy(mode_hbm.at[(chip + 1 + i) % 4], out, sem.at[i])
        for i, out in enumerate((m1_ref, m2_ref, m3_ref))
    ]
    for copy in copies:
        copy.start()
    zero = jnp.zeros((8, 56, NPTS), BF16)

    @pl.loop(0, NBLK // 8)
    def _(i):
        send_ref[pl.ds(i * 8, 8)] = zero
        head_ref[pl.ds(i * 8, 8)] = jnp.zeros((8, 8, NPTS), F32)

    @pl.loop(0, NBLK, unroll=16)
    def _(i):
        cnt_ref[i] = 0

    row = lax.broadcasted_iota(jnp.int32, (4, NPTS), 0)

    @pl.loop(0, NBLK, unroll=8)
    def _(b):
        o = own_ref[b]
        r = cnt_ref[o]
        cnt_ref[o] = r + 1
        r = jnp.minimum(r, 1)
        slot_ref[b] = o * 2 + r
        at = pl.multiple_of(b * NPTS, NPTS)
        v = jnp.broadcast_to(corner_ref[pl.ds(b, 1), :], (4, NPTS))
        vx = div_const(v, 49)
        rest = v - vx * 49
        vy = div_const(rest, 7)
        vz = rest - vy * 7
        head = jnp.where(
            row == 0, vx, jnp.where(row == 1, vy, jnp.where(row == 2, vz, cell_ref[b] + 1))
        )
        send_ref[o, pl.ds(pl.multiple_of(r * 16, 16), 16), :] = feat_ref[:, pl.ds(at, NPTS)]
        send_ref[o, pl.ds(pl.multiple_of(32 + r * 8, 8), 8), :] = w_ref[:, pl.ds(at, NPTS)]
        head_ref[o, pl.ds(r * 4, 4), :] = head.astype(F32)

    @pl.loop(0, NBLK // 8)
    def _(i):
        send_ref[pl.ds(i * 8, 8), 48:56, :] = head_ref[pl.ds(i * 8, 8)].astype(BF16)

    for copy in copies:
        copy.wait()


def pack(row, owner, cell, features, weights, corner, modes):
    smem = pl.BlockSpec(memory_space=pltpu.SMEM)
    vmem = pl.BlockSpec(memory_space=pltpu.VMEM)
    hbm = pl.BlockSpec(memory_space=pl.ANY)
    part = jax.ShapeDtypeStruct((8, CH, CH, 128), BF16)
    return pl.pallas_call(
        pack_kernel,
        out_shape=(
            jax.ShapeDtypeStruct((NBLK, 56, NPTS), BF16),
            jax.ShapeDtypeStruct((NBLK,), jnp.int32),
            part,
            part,
            part,
        ),
        in_specs=[smem, smem, smem, vmem, vmem, vmem, hbm],
        out_specs=(vmem, smem, vmem, vmem, vmem),
        scratch_shapes=[
            pltpu.SMEM((NBLK,), jnp.int32),
            pltpu.VMEM((NBLK, 8, NPTS), F32),
            pltpu.SemaphoreType.DMA((3,)),
        ],
        name="pack",
    )(row, owner, cell, features, weights, corner, modes)


def yz_basis(w, head):
    zi = lax.broadcasted_iota(jnp.int32, (8, NPTS), 0).astype(F32)
    bc = lambda k: jnp.broadcast_to(w[k : k + 1, :], (8, NPTS))
    vy = jnp.broadcast_to(head[1:2, :], (8, NPTS))
    vz = jnp.broadcast_to(head[2:3, :], (8, NPTS))
    m0 = zi == vz
    m1 = zi == vz + 1.0
    zero = jnp.zeros((8, NPTS), F32)
    zc = [
        [
            jnp.where(m0, bc(4 * dx + 2 * dy), jnp.where(m1, bc(4 * dx + 2 * dy + 1), zero))
            for dy in range(2)
        ]
        for dx in range(2)
    ]
    my = [vy == float(y) for y in range(7)]
    halves = []
    for dx in range(2):
        rows = []
        for y in range(8):
            val = zero
            if y > 0:
                val = jnp.where(my[y - 1], zc[dx][1], val)
            if y < 7:
                val = jnp.where(my[y], zc[dx][0], val)
            rows.append(val)
        halves.append(jnp.concatenate(rows, 0).astype(BF16))
    return jnp.concatenate(halves, 1)


def split_lanes(a, b):
    low = lax.broadcasted_iota(jnp.int32, a.shape, a.ndim - 1) < 64
    first = jnp.where(low, a, pltpu.roll(b, 64, a.ndim - 1))
    second = jnp.where(low, pltpu.roll(a, 64, a.ndim - 1), b)
    return first, second


def scatter_kernel(
    recv_hbm, tz_ref, field_hbm, out_hbm, ids_ref,
    recv_ref, g_ref, z_ref, field_ref, out_ref, in_sem, field_sem, out_sem, *, unroll
):
    part = NBLK // 4

    def fetch(k):
        at = pl.ds(k * part, part)
        return pltpu.make_async_copy(recv_hbm.at[at], recv_ref.at[at], in_sem.at[k])

    for k in range(4):
        fetch(k).start()
    zero = jnp.zeros((4, 64, 128), F32)

    @pl.loop(0, 64)
    def _(i):
        g_ref[pl.ds(i * 4, 4)] = zero

    @pl.loop(0, 4)
    def _(k):
        fetch(k).wait()

        @pl.loop(0, part // unroll)
        def _(i):
            for u in range(unroll):
                d = k * part + i * unroll + u
                weights = recv_ref[d, 32:48, :].astype(F32)
                heads = recv_ref[d, 48:56, :].astype(F32)
                for j in range(2):
                    head = heads[4 * j : 4 * j + 4]
                    basis = yz_basis(weights[8 * j : 8 * j + 8], head)
                    feat = recv_ref[d, 16 * j : 16 * j + 16, :].astype(F32)
                    vx = jnp.broadcast_to(head[0:1, :], (8, NPTS))
                    zf = jnp.zeros((8, NPTS), F32)
                    low, high = [], []
                    for ch in range(2):
                        half = feat[ch * 8 : ch * 8 + 8]
                        sel = [jnp.where(vx == float(x), half, 0.0) for x in range(7)]
                        low += sel + [zf]
                        high += [zf] + sel
                    lhs = jnp.concatenate(
                        [
                            jnp.concatenate(low, 0).astype(BF16),
                            jnp.concatenate(high, 0).astype(BF16),
                        ],
                        1,
                    )
                    res = mm(basis, lhs, NT)
                    b = jnp.clip(head[3, 0].astype(jnp.int32) - 1, 0, 255)
                    ids_ref[2 * d + j] = b
                    g_ref[b] = g_ref[b] + res

    tz = tz_ref[...]

    def put_field(q):
        at = pl.ds(q * 8, 8)
        return pltpu.make_async_copy(field_ref.at[at], field_hbm.at[at], field_sem.at[q])

    def put_out(s):
        return pltpu.make_async_copy(out_ref.at[s], out_hbm.at[:, s], out_sem.at[s])

    @pl.loop(0, 8, unroll=2)
    def _(q):
        bx = q // 2
        by = q % 2
        for h in range(4):
            ms = []
            for yl in (2 * h, 2 * h + 1):
                m = g_ref[pl.ds(q * 32, 32), yl * 8 : yl * 8 + 8, :].reshape(GRID, 128)
                m = m.astype(BF16)
                field_ref[q * 8 + yl] = m
                ms.append(m)
            res = mm(tz, jnp.concatenate(ms, 1))
            for e in range(2):
                y = by * 8 + 2 * h + e
                z_ref[bx, pl.ds(y, 128, stride=16), :] = res[:, e * 128 : e * 128 + 128]
        put_field(q).start()

    @pl.loop(0, 16, unroll=4)
    def _(s):
        for kz in range(4):
            for ri in range(2):
                at = pl.multiple_of(s * 128 + kz * 32 + ri * 16, 16)
                for p in range(2):
                    pair = split_lanes(
                        z_ref[2 * p, pl.ds(at, 16), :], z_ref[2 * p + 1, pl.ds(at, 16), :]
                    )
                    for ch in range(2):
                        out_ref[s, 2 * kz + ch, ri, p] = pair[ch].astype(BF16)
        put_out(s).start()

    @pl.loop(0, 8)
    def _(q):
        put_field(q).wait()

    @pl.loop(0, 16)
    def _(s):
        put_out(s).wait()


def scatter(recv, tz):
    smem = pl.BlockSpec(memory_space=pltpu.SMEM)
    vmem = pl.BlockSpec(memory_space=pltpu.VMEM)
    hbm = pl.BlockSpec(memory_space=pl.ANY)
    return pl.pallas_call(
        partial(scatter_kernel, unroll=16),
        out_shape=(
            jax.ShapeDtypeStruct((64, GRID, 128), BF16),
            jax.ShapeDtypeStruct((8, 16, 2, 2, 16, 128), BF16),
            jax.ShapeDtypeStruct((NSLOT,), jnp.int32),
        ),
        in_specs=[hbm, vmem],
        out_specs=(hbm, hbm, smem),
        scratch_shapes=[
            pltpu.VMEM((NBLK, 56, NPTS), BF16),
            pltpu.VMEM((256, 64, 128), F32),
            pltpu.VMEM((4, 2048, 128), F32),
            pltpu.VMEM((64, GRID, 128), BF16),
            pltpu.VMEM((16, 8, 2, 2, 16, 128), BF16),
            pltpu.SemaphoreType.DMA((4,)),
            pltpu.SemaphoreType.DMA((8,)),
            pltpu.SemaphoreType.DMA((16,)),
        ],
        name="scatter_z",
    )(recv, tz)


def group_transpose(x):
    n = x.shape[0]
    low, high = x[:, 0:8], x[:, 8:16]
    even = (lax.broadcasted_iota(jnp.int32, low.shape, 2) // 8) % 2 == 0
    first = jnp.where(even, low, pltpu.roll(high, 8, 2))
    second = jnp.where(even, pltpu.roll(low, 120, 2), high)
    x = jnp.concatenate([first, second], 0)
    group = lax.broadcasted_iota(jnp.int32, x.shape, 2) // 16
    x = pltpu.roll(x, 0, 2, stride=16, stride_axis=1)
    for k in range(3):
        d = 1 << k
        x = jnp.where((group // d) % 2 == 1, pltpu.roll(x, 8 - d, 1), x)
    x = pltpu.roll(x, 0, 2, stride=16, stride_axis=1)
    return jnp.concatenate([x[:n], x[n:]], 1)


def yx_kernel(row_ref, in_hbm, ty_ref, tx_ref, keep_ref, send_ref, in_ref, v_ref, sem):
    def get(r):
        at = pl.ds(r * COLS, COLS)
        return pltpu.make_async_copy(in_hbm.at[at], in_ref.at[at], sem.at[r])

    for r in range(8):
        get(r).start()

    @pl.loop(0, 8, unroll=2)
    def _(r):
        get(r).wait()
        at = pl.ds(r * COLS, COLS)
        rhs = jnp.concatenate([in_ref[at, :, p].reshape(512, 128) for p in range(2)], 1)
        res = mm(ty_ref[...], rhs)
        for p in range(2):
            tiles = group_transpose(res[:, p * 128 : p * 128 + 128].reshape(8, 16, 128))
            tiles = tiles.reshape(4, 32, 128).astype(BF16)
            to = pl.multiple_of(r * 64 + p * 32, 32)
            for g in range(4):
                v_ref[g, pl.ds(to, 32), :] = tiles[g]

    first = row_ref[0] % 2 == 0
    for g in range(4):
        spec = mm(tx_ref[...], v_ref[g]).T
        keep, send = choose(first, spec[0:64], spec[64:128])
        keep_ref[g] = keep.astype(BF16)
        send_ref[g] = send.astype(BF16)


def choose(first, a, b):
    return jnp.where(first, a, b), jnp.where(first, b, a)


def yx_forward(row, zs, ty, tx):
    smem = pl.BlockSpec(memory_space=pltpu.SMEM)
    vmem = pl.BlockSpec(memory_space=pltpu.VMEM)
    hbm = pl.BlockSpec(memory_space=pl.ANY)
    return pl.pallas_call(
        yx_kernel,
        out_shape=(jax.ShapeDtypeStruct((4, 64, 128), BF16),) * 2,
        in_specs=[smem, hbm, vmem, vmem],
        out_specs=(vmem, vmem),
        scratch_shapes=[
            pltpu.VMEM((128, 2, 2, 16, 128), BF16),
            pltpu.VMEM((4, 512, 128), BF16),
            pltpu.SemaphoreType.DMA((8,)),
        ],
        name="yx_forward",
    )(row, zs, ty, tx)


def mix_kernel(
    row_ref, own_ref, got_ref, mode_hbm, m1_hbm, m2_hbm, m3_hbm, keep_ref, send_ref, w_ref, sem
):
    chip = row_ref[0] // 2
    first = row_ref[0] % 2 == 0
    copies = [
        pltpu.make_async_copy(src, w_ref.at[d], sem.at[d])
        for d, src in enumerate((mode_hbm.at[chip], m1_hbm, m2_hbm, m3_hbm))
    ]
    for copy in copies:
        copy.start()
    lane = lax.broadcasted_iota(jnp.int32, (16, 128), 1)

    for d in range(4):
        copies[d].wait()
        j = (chip + 4 - d) % 4
        spec = choose(first, own_ref[j].astype(F32), got_ref[j].astype(F32))
        swapped = [pltpu.roll(x, 64, 1) for x in spec]
        halves = [[], []]
        for ky in range(8):
            a1 = jnp.zeros((16, 128), F32)
            a2 = jnp.zeros((16, 128), F32)
            for c in range(CH):
                w = w_ref[d, ky, c].astype(F32)
                at = ky * 8 + c % 8
                a1 = a1 + spec[c // 8][at : at + 1, :] * w
                a2 = a2 + swapped[c // 8][at : at + 1, :] * w
            res = jnp.where(lane < 64, a1 - pltpu.roll(a1, 64, 1), a2 + pltpu.roll(a2, 64, 1))
            for h in range(2):
                halves[h].append(res[h * 8 : h * 8 + 8])
        keep, send = choose(first, *[jnp.concatenate(half, 0) for half in halves])
        keep_ref[j] = keep.astype(BF16)
        send_ref[j] = send.astype(BF16)


def mix(row, own, got, modes, parts):
    smem = pl.BlockSpec(memory_space=pltpu.SMEM)
    vmem = pl.BlockSpec(memory_space=pltpu.VMEM)
    hbm = pl.BlockSpec(memory_space=pl.ANY)
    return pl.pallas_call(
        mix_kernel,
        out_shape=(jax.ShapeDtypeStruct((4, 64, 128), BF16),) * 2,
        in_specs=[smem, vmem, vmem, hbm, hbm, hbm, hbm],
        out_specs=(vmem, vmem),
        scratch_shapes=[
            pltpu.VMEM((4, 8, CH, CH, 128), BF16),
            pltpu.SemaphoreType.DMA((4,)),
        ],
        name="mix",
    )(row, own, got, modes, *parts)


def xy_kernel(row_ref, own_ref, got_ref, ix_ref, iy_ref, out_hbm, u_ref, out_ref, sem):
    def put(r):
        at = pl.ds(r * COLS, COLS)
        return pltpu.make_async_copy(out_ref.at[at], out_hbm.at[at], sem.at[r])

    @pl.loop(0, 4, unroll=2)
    def _(g):
        pair = choose(row_ref[0] % 2 == 0, own_ref[g].astype(F32), got_ref[g].astype(F32))
        rhs = jnp.concatenate(pair, 0).astype(BF16)
        xi = group_transpose(mm(ix_ref[...], rhs, NT).reshape(32, 16, 128))
        u_ref[g] = xi.astype(BF16)

    @pl.loop(0, 8, unroll=2)
    def _(r):
        rhs = jnp.concatenate(
            [u_ref[:, pl.ds(r * 4 + p * 2, 2)].reshape(128, 128) for p in range(2)], 1
        )
        res = mm(iy_ref[...], rhs).astype(BF16)
        for s in range(16):
            for ri in range(2):
                at = s * 32 + ri * 16
                for p in range(2):
                    out_ref[r * COLS + s, ri, p] = res[at : at + 16, p * 128 : p * 128 + 128]
        put(r).start()

    for r in range(8):
        put(r).wait()


def xy_inverse(row, own, got, ix, iy):
    smem = pl.BlockSpec(memory_space=pltpu.SMEM)
    vmem = pl.BlockSpec(memory_space=pltpu.VMEM)
    hbm = pl.BlockSpec(memory_space=pl.ANY)
    return pl.pallas_call(
        xy_kernel,
        out_shape=jax.ShapeDtypeStruct((128, 2, 2, 16, 128), BF16),
        in_specs=[smem, vmem, vmem, vmem, vmem],
        out_specs=hbm,
        scratch_shapes=[
            pltpu.VMEM((4, 32, 16, 128), BF16),
            pltpu.VMEM((128, 2, 2, 16, 128), BF16),
            pltpu.SemaphoreType.DMA((8,)),
        ],
        name="xy_inverse",
    )(row, own, got, ix, iy)


def gelu(x):
    x = x.astype(BF16)
    c = math.sqrt(2.0 / math.pi)
    t = jnp.tanh(x * (jnp.asarray(c, BF16) + jnp.asarray(c * 0.044715, BF16) * (x * x)))
    h = x * jnp.asarray(0.5, BF16)
    return h + h * t


def expand_weights(in_ref, skip_ref, out_ref, w1_ref, w2_ref):
    iota = lambda shape, d: lax.broadcasted_iota(jnp.int32, shape, d)
    hot = lambda cond: jnp.where(cond, 1.0, 0.0).astype(BF16)
    rep = hot(iota((HID, 512), 0) == iota((HID, 512), 1) % HID)
    row = iota((128, CH), 0)
    chan = hot((row // 64) * 8 + row % 8 == iota((128, CH), 1))
    keep = (iota((128, 512), 0) // 8) % 8 == iota((128, 512), 1) // HID
    first = in_ref[...]
    both = mm(skip_ref[...], first, TN).astype(BF16)
    for e, w in enumerate((first, both)):
        full = mm(chan, mm(w, rep).astype(BF16))
        w1_ref[e * 128 : e * 128 + 128, :] = jnp.where(keep, full, 0.0).astype(BF16)
    rows = hot(iota((512, HID), 0) % HID == iota((512, HID), 1))
    cols = hot(iota((CH, 128), 1) % CH == iota((CH, 128), 0))
    full = mm(mm(rows, out_ref[...], NT).astype(BF16), cols)
    keep = iota((512, 128), 0) // HID == iota((512, 128), 1) // CH
    w2_ref[...] = jnp.where(keep, full, 0.0).astype(BF16)


def final_kernel(
    ids_ref, yi_hbm, field_hbm, recv_hbm, iz_ref, in_ref, skip_ref, bias_ref, mout_ref, out_hbm,
    yi_ref, field_ref, tail_ref, out_ref, y_ref, xa_ref, xb_ref, l_ref, w1_ref, w2_ref, b1_ref,
    yi_sem, field_sem, tail_sem, out_sem, *, ny, unroll
):
    def get_yi(r):
        at = pl.ds(r * COLS, COLS)
        return pltpu.make_async_copy(yi_hbm.at[at], yi_ref.at[at], yi_sem.at[r])

    def put_out(i):
        at = pl.ds(i * 2 * unroll, 2 * unroll)
        return pltpu.make_async_copy(out_ref.at[at], out_hbm.at[at], out_sem.at[i])

    get_field = pltpu.make_async_copy(field_hbm, field_ref, field_sem)
    get_tail = pltpu.make_async_copy(recv_hbm.at[:, 32:56], tail_ref, tail_sem)

    @pl.loop(0, 8)
    def _(r):
        get_yi(r).start()

    get_field.start()
    get_tail.start()
    expand_weights(in_ref, skip_ref, mout_ref, w1_ref, w2_ref)
    b1_ref[...] = jnp.concatenate([bias_ref[...]] * 8, 1)

    @pl.loop(0, 4)
    def _(kz):
        get_yi(2 * kz).wait()
        get_yi(2 * kz + 1).wait()

        @pl.loop(0, 16, unroll=4)
        def _(s):
            for ri in range(2):
                at = pl.multiple_of(s * 128 + kz * 32 + ri * 16, 16)
                for p in range(2):
                    pair = split_lanes(
                        yi_ref[kz * 32 + s, ri, p].astype(F32),
                        yi_ref[kz * 32 + 16 + s, ri, p].astype(F32),
                    )
                    for e in range(2):
                        y_ref[2 * p + e, pl.ds(at, 16), :] = pair[e]

    def stage(i, x_ref):
        base = i * ny
        bx = base // 16
        for p in range(ny // 2):
            y = (base + 2 * p) % 16
            rhs = jnp.concatenate(
                [y_ref[bx, pl.ds(y + e, 128, stride=16), :] for e in range(2)], 1
            ).astype(BF16)
            res = mm(iz_ref[...], rhs).astype(BF16)
            for e in range(2):
                at = (2 * p + e) * GRID
                x_ref[at : at + GRID, 0:128] = res[:, e * 128 : e * 128 + 128]
                x_ref[at : at + GRID, 128:256] = field_ref[base + 2 * p + e]

    def layer(i, x_ref):
        h = gelu(mm(x_ref[...], w1_ref[...]) + b1_ref[...])
        o = mm(h, w2_ref[...]).astype(BF16).astype(F32)
        l_ref[pl.ds(i * ny, ny)] = o.reshape(ny, GRID, 128)

    steps = 64 // ny
    get_field.wait()
    stage(0, xa_ref)

    @pl.loop(0, steps // 2)
    def _(i):
        stage(2 * i + 1, xb_ref)
        layer(2 * i, xa_ref)
        stage(jnp.minimum(2 * i + 2, steps - 1), xa_ref)
        layer(2 * i + 1, xb_ref)

    get_tail.wait()

    @pl.loop(0, NBLK // unroll)
    def _(i):
        for u in range(unroll):
            d = i * unroll + u
            weights = tail_ref[d, 0:16, :].astype(F32)
            heads = tail_ref[d, 16:24, :].astype(F32)
            for j in range(2):
                head = heads[4 * j : 4 * j + 4]
                basis = yz_basis(weights[8 * j : 8 * j + 8], head)
                b = ids_ref[2 * d + j]
                q = b // 32
                at = pl.multiple_of((b % 32) * 8, 8)
                cells = l_ref[pl.ds(q * 8, 8), pl.ds(at, 8), :].reshape(64, 128).astype(BF16)
                res = mm(cells, basis, TN)
                vx = jnp.broadcast_to(head[0:1, :], (16, NPTS))
                val = jnp.zeros((16, NPTS), F32)
                for x in range(7):
                    got = (
                        res[x * 16 : x * 16 + 16, 0:128]
                        + res[x * 16 + 16 : x * 16 + 32, 128:256]
                    )
                    val = jnp.where(vx == float(x), got, val)
                out_ref[2 * d + j] = val.astype(BF16)
        put_out(i).start()

    @pl.loop(0, NBLK // unroll)
    def _(i):
        put_out(i).wait()


def final(ids, yi, field, recv, iz, first, skip, bias, mout):
    smem = pl.BlockSpec(memory_space=pltpu.SMEM)
    vmem = pl.BlockSpec(memory_space=pltpu.VMEM)
    hbm = pl.BlockSpec(memory_space=pl.ANY)
    ny, unroll = 8, 16
    return pl.pallas_call(
        partial(final_kernel, ny=ny, unroll=unroll),
        out_shape=jax.ShapeDtypeStruct((NSLOT, 16, NPTS), BF16),
        in_specs=[smem, hbm, hbm, hbm, vmem, vmem, vmem, vmem, vmem],
        out_specs=hbm,
        scratch_shapes=[
            pltpu.VMEM((128, 2, 2, 16, 128), BF16),
            pltpu.VMEM((64, GRID, 128), BF16),
            pltpu.VMEM((NBLK, 24, NPTS), BF16),
            pltpu.VMEM((NSLOT, 16, NPTS), BF16),
            pltpu.VMEM((4, 2048, 128), F32),
            pltpu.VMEM((ny * GRID, 256), BF16),
            pltpu.VMEM((ny * GRID, 256), BF16),
            pltpu.VMEM((64, GRID, 128), F32),
            pltpu.VMEM((256, 512), BF16),
            pltpu.VMEM((512, 128), BF16),
            pltpu.VMEM((1, 512), F32),
            pltpu.SemaphoreType.DMA((8,)),
            pltpu.SemaphoreType.DMA,
            pltpu.SemaphoreType.DMA,
            pltpu.SemaphoreType.DMA((NBLK // unroll,)),
        ],
        name="mlp_gather",
    )(ids, yi, field, recv, iz, first, skip, bias, mout)


def unpack_kernel(slot_ref, in_ref, out_ref):
    @pl.loop(0, NBLK, unroll=8)
    def _(b):
        at = pl.multiple_of(b * NPTS, NPTS)
        out_ref[:, pl.ds(at, NPTS)] = in_ref[slot_ref[b]]


def unpack(slots, vals):
    smem = pl.BlockSpec(memory_space=pltpu.SMEM)
    vmem = pl.BlockSpec(memory_space=pltpu.VMEM)
    return pl.pallas_call(
        unpack_kernel,
        out_shape=jax.ShapeDtypeStruct((CH, NBLK * NPTS), BF16),
        in_specs=[smem, vmem],
        out_specs=vmem,
        name="unpack",
    )(slots, vals)


def a2a(x, axes):
    return lax.all_to_all(x, axes, split_axis=0, concat_axis=0, tiled=True)


def partner(x):
    return lax.ppermute(x, "row", [(i, i ^ 1) for i in range(ROWS)])


def body(
    features,
    point_weights,
    point_corner,
    block_owner,
    block_cell,
    spec_weight,
    skip_weight,
    mlp_in,
    mlp_bias,
    mlp_out,
):
    tz, ty, tx, ix, iy, iz = tables()
    owner = block_owner.reshape(NBLK)
    row = lax.axis_index("row").astype(jnp.int32)[None]
    corner = point_corner.reshape(NBLK, NPTS)
    send, slots, *parts = pack(
        row, owner, block_cell, features, point_weights, corner, spec_weight
    )
    parts = [
        lax.ppermute(part, "row", [(i, (i + 2 * d) % ROWS) for i in range(ROWS)])
        for d, part in zip((1, 2, 3), parts)
    ]
    recv = a2a(send, ("row", "col"))
    field, zs, ids = scatter(recv, tz)
    zs = a2a(zs.reshape(128, 2, 2, 16, 128), ("row", "col"))
    keep, send = yx_forward(row, zs, ty, tx)
    keep, send = mix(row, keep, partner(send), spec_weight, parts)
    yi = a2a(xy_inverse(row, keep, partner(send), ix, iy), ("row", "col"))
    vals = final(
        ids, yi, field, recv, iz, mlp_in.T, skip_weight, mlp_bias.reshape(1, HID), mlp_out
    )
    return unpack(slots, a2a(vals, ("row", "col")))


def solution(mesh):
    return jax.shard_map(
        body,
        mesh=mesh,
        in_specs=(
            P(None, ("row", "col")),
            P(None, ("row", "col")),
            P(("row", "col")),
            P(("row", "col"), None),
            P(("row", "col")),
            P("col", "row", None, None, None),
            P(),
            P(),
            P(),
            P(),
        ),
        out_specs=P(None, ("row", "col")),
        check_vma=False,
    )
```

profile of v0, /device:TPU:1, one launch (start us, length us, event | category | flops | bytes accessed | tf_op | source)
XLA Modules:
  0.0 209.1 jit_solution(13184869486115999182)
XLA Ops:
  0.0 4.9 %pack.1 = (bf16[128,56,128]{2,1,0:T(8,128)(2,1)}, s32[128]{0:T(128)}, bf16[8,16,16,128]{3,2,1,0:T(8,128)(2,1)}, bf16[8,16,16,128]{3,2,1,0:T(8,128)(2,1)}, bf16[8,16,16,128]{3,2,1,0:T(8,128)(2,1)}) custom-call(s32[1]{0:T(128)} %bitcast.row_ref, s32[128]{0:T(128)} %bitcast.9, s32[128]{0:T(128)} %cell_ref.1, bf16[16,16384]{1,0:T(8,128)(2,1)} %feat_ref.1, ...), custom_call_target="tpu_custom_call" | custom-call | tf_op jit(solution)/shard_map/pack/pallas_call | solution.py:130
  4.9 38.4 %all_to_all.20.recv_hbm = bf16[128,56,128]{2,1,0:T(8,128)(2,1)} all-to-all(bf16[128,56,128]{2,1,0:T(8,128)(2,1)} %get-tuple-element.18), channel_id=1, replica_groups=mesh['row'=8,'col'=16] {'row','col'}, dimensions={0} | all-to-all | bytes 3670016 | tf_op jit(solution)/shard_map/all_to_all | solution.py:662
  43.2 13.2 %scatter_z.1 = (bf16[64,256,128]{2,1,0:T(8,128)(2,1)}, bf16[8,16,2,2,16,128]{5,4,3,2,1,0:T(8,128)(2,1)}, s32[256]{0:T(256)}) custom-call(bf16[128,56,128]{2,1,0:T(8,128)(2,1)} %all_to_all.20.recv_hbm, bf16[128,256]{1,0:T(8,128)(2,1)} %constant.25.tz_ref), custom_call_target="tpu_custom_call" | custom-call | tf_op jit(solution)/shard_map/scatter_z/pallas_call | solution.py:291
  56.5 4.9 %all-to-all-start.1 = ((bf16[128,2,2,16,128]{4,3,2,1,0:T(8,128)(2,1)}), bf16[128,2,2,16,128]{4,3,2,1,0:T(8,128)(2,1)S(1)}, u32[]{:S(2)}, u32[]{:S(2)}) async-start(bf16[128,2,2,16,128]{4,3,2,1,0:T(8,128)(2,1)} %bitcast.6), calls=%async_computation.1 | async-start | bytes 4194304 | tf_op jit(solution)/shard_map/all_to_all | solution.py:662
  61.4 1.5 collective-permute-start.1
  62.9 2.5 %collective-permute-start.2 = (bf16[8,16,16,128]{3,2,1,0:T(8,128)(2,1)}, bf16[8,16,16,128]{3,2,1,0:T(8,128)(2,1)S(1)}, u32[]{:S(2)}, u32[]{:S(2)}) collective-permute-start(bf16[8,16,16,128]{3,2,1,0:T(8,128)(2,1)} %get-tuple-element.24), channel_id=1, source_target_pairs={{0,64},{16,80},{32,96},{48,112},{64,0},{80,16},{96,32},{112,48},{1... | collective-permute-start | bytes 1572872 | tf_op jit(solution)/shard_map/ppermute | solution.py:689
  65.4 1.1 collective-permute-start.3
  66.5 24.4 %all-to-all-done.1.in_hbm = bf16[128,2,2,16,128]{4,3,2,1,0:T(8,128)(2,1)S(1)} async-done(((bf16[128,2,2,16,128]{4,3,2,1,0:T(8,128)(2,1)}), bf16[128,2,2,16,128]{4,3,2,1,0:T(8,128)(2,1)S(1)}, u32[]{:S(2)}, u32[]{:S(2)}) %all-to-all-start.1) | async-done | bytes 2097184 | tf_op jit(solution)/shard_map/all_to_all | solution.py:662
  91.0 1.3 copy-done
  92.3 6.5 %yx_forward.1 = (bf16[4,64,128]{2,1,0:T(8,128)(2,1)}, bf16[4,64,128]{2,1,0:T(8,128)(2,1)}) custom-call(s32[1]{0:T(128)} %bitcast.row_ref, bf16[128,2,2,16,128]{4,3,2,1,0:T(8,128)(2,1)} %copy-done, bf16[128,512]{1,0:T(8,128)(2,1)} %constant.26.ty_ref, bf16[128,512]{1,0:T(8,128)(2,1)} %constant.27.tx_ref), custom_call_target="tpu_custom_call" | custom-call | tf_op jit(solution)/shard_map/yx_forward/pallas_call | solution.py:367
  98.8 1.5 collective-permute-start
  100.3 0.0 collective-permute-done.1.m1_hbm
  100.3 9.0 %collective-permute-done.2.m2_hbm = bf16[8,16,16,128]{3,2,1,0:T(8,128)(2,1)S(1)} collective-permute-done((bf16[8,16,16,128]{3,2,1,0:T(8,128)(2,1)}, bf16[8,16,16,128]{3,2,1,0:T(8,128)(2,1)S(1)}, u32[]{:S(2)}, u32[]{:S(2)}) %collective-permute-start.2) | collective-permute-done | bytes 524320 | tf_op jit(solution)/shard_map/ppermute | solution.py:689
  109.4 0.8 copy-done.2
  110.1 0.0 copy-done.3
  110.2 3.8 %mix.1 = (bf16[4,64,128]{2,1,0:T(8,128)(2,1)}, bf16[4,64,128]{2,1,0:T(8,128)(2,1)}) custom-call(s32[1]{0:T(128)} %bitcast.row_ref, bf16[4,64,128]{2,1,0:T(8,128)(2,1)} %get-tuple-element.21.own_ref, bf16[4,64,128]{2,1,0:T(8,128)(2,1)} %copy-done.3, bf16[4,8,16,16,128]{4,3,2,1,0:T(8,128)(2,1)} %mode_hbm.3, bf16[8,16,16,128]{3,2,1,0:T(8,128)(2,1)} %copy-done.1, ...), custom_call_target="tpu_custom_call" | custom-call | tf_op jit(solution)/shard_map/mix/pallas_call | solution.py:420
  114.0 1.0 collective-permute-start.4
  115.0 1.1 collective-permute-done.4.got_ref
  116.2 0.6 copy-done.4
  116.8 4.2 %xy_inverse.1 = bf16[128,2,2,16,128]{4,3,2,1,0:T(8,128)(2,1)} custom-call(s32[1]{0:T(128)} %bitcast.row_ref, bf16[4,64,128]{2,1,0:T(8,128)(2,1)} %get-tuple-element.26.own_ref, bf16[4,64,128]{2,1,0:T(8,128)(2,1)} %copy-done.4, bf16[512,128]{1,0:T(8,128)(2,1)} %constant.28.ix_ref, bf16[512,128]{1,0:T(8,128)(2,1)} %constant.29.iy_ref), custom_call_target="tpu_custom_call" | custom-call | tf_op jit(solution)/shard_map/xy_inverse/pallas_call | solution.py:466
  121.0 37.2 %all_to_all.21.yi_hbm = bf16[128,2,2,16,128]{4,3,2,1,0:T(8,128)(2,1)} all-to-all(bf16[128,2,2,16,128]{4,3,2,1,0:T(8,128)(2,1)} %xy_inverse.1), channel_id=1, replica_groups=mesh['row'=8,'col'=16] {'row','col'}, dimensions={0} | all-to-all | bytes 4194304 | tf_op jit(solution)/shard_map/all_to_all | solution.py:662
  158.2 23.2 %mlp_gather.1 = bf16[256,16,128]{2,1,0:T(8,128)(2,1)} custom-call(s32[256]{0:T(256)} %get-tuple-element.19.ids_ref, bf16[128,2,2,16,128]{4,3,2,1,0:T(8,128)(2,1)} %all_to_all.21.yi_hbm, bf16[64,256,128]{2,1,0:T(8,128)(2,1)} %get-tuple-element.28.field_hbm, bf16[128,56,128]{2,1,0:T(8,128)(2,1)} %all_to_all.20.recv_hbm, bf16[256,128]{1,0:T(8,128)(2,1)} %constant.30.iz_ref, ...), custom_call_target="tpu_custom_call" | custom-call | tf_op jit(solution)/shard_map/mlp_gather/pallas_call | solution.py:616
  181.4 25.3 %all_to_all.22.in_ref = bf16[256,16,128]{2,1,0:T(8,128)(2,1)} all-to-all(bf16[256,16,128]{2,1,0:T(8,128)(2,1)} %mlp_gather.1), channel_id=1, replica_groups=mesh['row'=8,'col'=16] {'row','col'}, dimensions={0} | all-to-all | bytes 2097152 | tf_op jit(solution)/shard_map/all_to_all | solution.py:662
  206.7 2.4 %unpack.1 = bf16[16,16384]{1,0:T(8,128)(2,1)} custom-call(s32[128]{0:T(128)} %get-tuple-element.17.slot_ref, bf16[256,16,128]{2,1,0:T(8,128)(2,1)} %all_to_all.22.in_ref), custom_call_target="tpu_custom_call" | custom-call | tf_op jit(solution)/shard_map/unpack/pallas_call | solution.py:652
  (8 shorter events, 0.0 us)
Async XLA Ops:
  56.5 34.5 %all-to-all-start.1 = ((bf16[128,2,2,16,128]{4,3,2,1,0:T(8,128)(2,1)}), bf16[128,2,2,16,128]{4,3,2,1,0:T(8,128)(2,1)S(1)}, u32[]{:S(2)}, u32[]{:S(2)}) async-start(bf16[128,2,2,16,128]{4,3,2,1,0:T(8,128)(2,1)} %bitcast.6), calls=%async_computation.1 | async-start | bytes 4194304 | tf_op jit(solution)/shard_map/all_to_all | solution.py:662
  61.4 38.9 %collective-permute-start.1 = (bf16[8,16,16,128]{3,2,1,0:T(8,128)(2,1)}, bf16[8,16,16,128]{3,2,1,0:T(8,128)(2,1)S(1)}, u32[]{:S(2)}, u32[]{:S(2)}) collective-permute-start(bf16[8,16,16,128]{3,2,1,0:T(8,128)(2,1)} %get-tuple-element.23), channel_id=1, source_target_pairs={{0,32},{16,48},{32,64},{48,80},{64,96},{80,112},{96,0},{112,16},{1... | collective-permute-start | bytes 1572872 | tf_op jit(solution)/shard_map/ppermute | solution.py:689
  62.9 46.5 %collective-permute-start.2 = (bf16[8,16,16,128]{3,2,1,0:T(8,128)(2,1)}, bf16[8,16,16,128]{3,2,1,0:T(8,128)(2,1)S(1)}, u32[]{:S(2)}, u32[]{:S(2)}) collective-permute-start(bf16[8,16,16,128]{3,2,1,0:T(8,128)(2,1)} %get-tuple-element.24), channel_id=1, source_target_pairs={{0,64},{16,80},{32,96},{48,112},{64,0},{80,16},{96,32},{112,48},{1... | collective-permute-start | bytes 1572872 | tf_op jit(solution)/shard_map/ppermute | solution.py:689
  65.4 43.9 %collective-permute-start.3 = (bf16[8,16,16,128]{3,2,1,0:T(8,128)(2,1)}, bf16[8,16,16,128]{3,2,1,0:T(8,128)(2,1)}, u32[]{:S(2)}, u32[]{:S(2)}) collective-permute-start(bf16[8,16,16,128]{3,2,1,0:T(8,128)(2,1)} %get-tuple-element.25), channel_id=1, source_target_pairs={{0,96},{16,112},{32,0},{48,16},{64,32},{80,48},{96,64},{112,80},{1... | collective-permute-start | bytes 1572872 | tf_op jit(solution)/shard_map/ppermute | solution.py:689
  91.0 1.3 copy-start
  98.8 10.5 %collective-permute-start = (bf16[4,64,128]{2,1,0:T(8,128)(2,1)}, bf16[4,64,128]{2,1,0:T(8,128)(2,1)S(1)}, u32[]{:S(2)}, u32[]{:S(2)}) collective-permute-start(bf16[4,64,128]{2,1,0:T(8,128)(2,1)} %get-tuple-element.22), channel_id=1, source_target_pairs={{0,16},{16,0},{32,48},{48,32},{64,80},{80,64},{96,112},{112,96},{1... | collective-permute-start | bytes 196616 | tf_op jit(solution)/shard_map/ppermute | solution.py:666
  100.3 9.1 %copy-start.1 = (bf16[8,16,16,128]{3,2,1,0:T(8,128)(2,1)}, bf16[8,16,16,128]{3,2,1,0:T(8,128)(2,1)S(1)}, u32[]{:S(2)}) copy-start(bf16[8,16,16,128]{3,2,1,0:T(8,128)(2,1)S(1)} %collective-permute-done.1.m1_hbm) | copy-start | bytes 1572868
  109.3 0.8 copy-start.2
  109.4 0.8 copy-start.3
  114.0 2.2 %collective-permute-start.4 = (bf16[4,64,128]{2,1,0:T(8,128)(2,1)}, bf16[4,64,128]{2,1,0:T(8,128)(2,1)S(1)}, u32[]{:S(2)}, u32[]{:S(2)}) collective-permute-start(bf16[4,64,128]{2,1,0:T(8,128)(2,1)} %get-tuple-element.27), channel_id=1, source_target_pairs={{0,16},{16,0},{32,48},{48,32},{64,80},{80,64},{96,112},{112,96},{1... | collective-permute-start | bytes 196616 | tf_op jit(solution)/shard_map/ppermute | solution.py:666
  116.2 0.6 copy-start.4
where the time goes:
time: 210 us; the launch traced here: 209 us
  blocking collectives  101 us (48%)
  Pallas kernels  58.1 us (28%)
  waiting for transfers between devices  34.6 us (16%)
  starting transfers between devices  12.6 us (6%)
  local copies, waits for them, and re-layouts  2.78 us (1%)
    all_to_all x3, blocking collectives, a2a(): return lax.all_to_all(x, axes, split_axis=0, concat_axis=0, tiled=True)  101 us
    all_to_all x1, waiting for transfers between devices, a2a(): return lax.all_to_all(x, axes, split_axis=0, concat_axis=0, tiled=True)  24.4 us
    pallas_call x1, Pallas kernels, final(): pl.pallas_call(partial(final_kernel, ny=ny, unroll=unroll), out_shape=jax...  23.2 us
    pallas_call x1, Pallas kernels, scatter(): pl.pallas_call(partial(scatter_kernel, unroll=16), out_shape=(jax.ShapeDt...  13.2 us
    ppermute x3, waiting for transfers between devices, body(): lax.ppermute(part, 'row', [(i, (i + 2 * d) % ROWS) for i in range(ROWS)])  9.03 us
    pallas_call x1, Pallas kernels, yx_forward(): pl.pallas_call(yx_kernel, out_shape=(jax.ShapeDtypeStruct((4, 64, 128), B...  6.5 us
    ppermute x3, starting transfers between devices, body(): lax.ppermute(part, 'row', [(i, (i + 2 * d) % ROWS) for i in range(ROWS)])  5.13 us
    all_to_all x1, starting transfers between devices, a2a(): return lax.all_to_all(x, axes, split_axis=0, concat_axis=0, tiled=True)  4.92 us
  transfers between devices with their start and end apart: 6, of which 3 were waited for; matrix products, arithmetic and copies ran while one was open for 0% of the time, Pallas kernels for 3%

commit v1 on v0

--- a/solution.py
+++ b/solution.py
@@ -23,6 +23,14 @@
 NN = (((1,), (0,)), ((), ()))
 NT = (((1,), (1,)), ((), ()))
 TN = (((0,), (0,)), ((), ()))
+
+
+def near(x):
+    return pltpu.with_memory_space_constraint(x, pltpu.VMEM)
+
+
+def grant(mib):
+    return pltpu.CompilerParams(vmem_limit_bytes=mib << 20)
 
 
 def mm(a, b, dims=NN):
@@ -125,12 +133,12 @@
 def pack(row, owner, cell, features, weights, corner, modes):
     smem = pl.BlockSpec(memory_space=pltpu.SMEM)
     vmem = pl.BlockSpec(memory_space=pltpu.VMEM)
-    hbm = pl.BlockSpec(memory_space=pl.ANY)
-    part = jax.ShapeDtypeStruct((8, CH, CH, 128), BF16)
+    hbm = pl.BlockSpec(memory_space=pltpu.HBM)
+    part = pltpu.HBM((8, CH, CH, 128), BF16)
     return pl.pallas_call(
         pack_kernel,
         out_shape=(
-            jax.ShapeDtypeStruct((NBLK, 56, NPTS), BF16),
+            pltpu.HBM((NBLK, 56, NPTS), BF16),
             jax.ShapeDtypeStruct((NBLK,), jnp.int32),
             part,
             part,
@@ -143,6 +151,7 @@
             pltpu.VMEM((NBLK, 8, NPTS), F32),
             pltpu.SemaphoreType.DMA((3,)),
         ],
+        compiler_params=grant(16),
         name="pack",
     )(row, owner, cell, features, weights, corner, modes)
 
@@ -185,65 +194,45 @@
 
 
 def scatter_kernel(
-    recv_hbm, tz_ref, field_hbm, out_hbm, ids_ref,
-    recv_ref, g_ref, z_ref, field_ref, out_ref, in_sem, field_sem, out_sem, *, unroll
+    recv_ref, tz_ref, field_ref, out_ref, ids_ref, g_ref, z_ref, *, unroll
 ):
-    part = NBLK // 4
-
-    def fetch(k):
-        at = pl.ds(k * part, part)
-        return pltpu.make_async_copy(recv_hbm.at[at], recv_ref.at[at], in_sem.at[k])
-
-    for k in range(4):
-        fetch(k).start()
     zero = jnp.zeros((4, 64, 128), F32)
 
     @pl.loop(0, 64)
     def _(i):
         g_ref[pl.ds(i * 4, 4)] = zero
 
-    @pl.loop(0, 4)
-    def _(k):
-        fetch(k).wait()
-
-        @pl.loop(0, part // unroll)
-        def _(i):
-            for u in range(unroll):
-                d = k * part + i * unroll + u
-                weights = recv_ref[d, 32:48, :].astype(F32)
-                heads = recv_ref[d, 48:56, :].astype(F32)
-                for j in range(2):
-                    head = heads[4 * j : 4 * j + 4]
-                    basis = yz_basis(weights[8 * j : 8 * j + 8], head)
-                    feat = recv_ref[d, 16 * j : 16 * j + 16, :].astype(F32)
-                    vx = jnp.broadcast_to(head[0:1, :], (8, NPTS))
-                    zf = jnp.zeros((8, NPTS), F32)
-                    low, high = [], []
-                    for ch in range(2):
-                        half = feat[ch * 8 : ch * 8 + 8]
-                        sel = [jnp.where(vx == float(x), half, 0.0) for x in range(7)]
-                        low += sel + [zf]
-                        high += [zf] + sel
-                    lhs = jnp.concatenate(
-                        [
-                            jnp.concatenate(low, 0).astype(BF16),
-                            jnp.concatenate(high, 0).astype(BF16),
-                        ],
-                        1,
-                    )
-                    res = mm(basis, lhs, NT)
-                    b = jnp.clip(head[3, 0].astype(jnp.int32) - 1, 0, 255)
-                    ids_ref[2 * d + j] = b
-                    g_ref[b] = g_ref[b] + res
+    @pl.loop(0, NBLK // unroll)
+    def _(i):
+        for u in range(unroll):
+            d = i * unroll + u
+            weights = recv_ref[d, 32:48, :].astype(F32)
+            heads = recv_ref[d, 48:56, :].astype(F32)
+            for j in range(2):
+                head = heads[4 * j : 4 * j + 4]
+                basis = yz_basis(weights[8 * j : 8 * j + 8], head)
+                feat = recv_ref[d, 16 * j : 16 * j + 16, :].astype(F32)
+                vx = jnp.broadcast_to(head[0:1, :], (8, NPTS))
+                zf = jnp.zeros((8, NPTS), F32)
+                low, high = [], []
+                for ch in range(2):
+                    half = feat[ch * 8 : ch * 8 + 8]
+                    sel = [jnp.where(vx == float(x), half, 0.0) for x in range(7)]
+                    low += sel + [zf]
+                    high += [zf] + sel
+                lhs = jnp.concatenate(
+                    [
+                        jnp.concatenate(low, 0).astype(BF16),
+                        jnp.concatenate(high, 0).astype(BF16),
+                    ],
+                    1,
+                )
+                res = mm(basis, lhs, NT)
+                b = jnp.clip(head[3, 0].astype(jnp.int32) - 1, 0, 255)
+                ids_ref[2 * d + j] = b
+                g_ref[b] = g_ref[b] + res
 
     tz = tz_ref[...]
-
-    def put_field(q):
-        at = pl.ds(q * 8, 8)
-        return pltpu.make_async_copy(field_ref.at[at], field_hbm.at[at], field_sem.at[q])
-
-    def put_out(s):
-        return pltpu.make_async_copy(out_ref.at[s], out_hbm.at[:, s], out_sem.at[s])
 
     @pl.loop(0, 8, unroll=2)
     def _(q):
@@ -260,7 +249,6 @@
             for e in range(2):
                 y = by * 8 + 2 * h + e
                 z_ref[bx, pl.ds(y, 128, stride=16), :] = res[:, e * 128 : e * 128 + 128]
-        put_field(q).start()
 
     @pl.loop(0, 16, unroll=4)
     def _(s):
@@ -272,41 +260,26 @@
                         z_ref[2 * p, pl.ds(at, 16), :], z_ref[2 * p + 1, pl.ds(at, 16), :]
                     )
                     for ch in range(2):
-                        out_ref[s, 2 * kz + ch, ri, p] = pair[ch].astype(BF16)
-        put_out(s).start()
-
-    @pl.loop(0, 8)
-    def _(q):
-        put_field(q).wait()
-
-    @pl.loop(0, 16)
-    def _(s):
-        put_out(s).wait()
+                        out_ref[2 * kz + ch, s, ri, p] = pair[ch].astype(BF16)
 
 
 def scatter(recv, tz):
     smem = pl.BlockSpec(memory_space=pltpu.SMEM)
     vmem = pl.BlockSpec(memory_space=pltpu.VMEM)
-    hbm = pl.BlockSpec(memory_space=pl.ANY)
     return pl.pallas_call(
         partial(scatter_kernel, unroll=16),
         out_shape=(
-            jax.ShapeDtypeStruct((64, GRID, 128), BF16),
-            jax.ShapeDtypeStruct((8, 16, 2, 2, 16, 128), BF16),
+            pltpu.VMEM((64, GRID, 128), BF16),
+            pltpu.VMEM((8, 16, 2, 2, 16, 128), BF16),
             jax.ShapeDtypeStruct((NSLOT,), jnp.int32),
         ),
-        in_specs=[hbm, vmem],
-        out_specs=(hbm, hbm, smem),
+        in_specs=[vmem, vmem],
+        out_specs=(vmem, vmem, smem),
         scratch_shapes=[
-            pltpu.VMEM((NBLK, 56, NPTS), BF16),
             pltpu.VMEM((256, 64, 128), F32),
             pltpu.VMEM((4, 2048, 128), F32),
-            pltpu.VMEM((64, GRID, 128), BF16),
-            pltpu.VMEM((16, 8, 2, 2, 16, 128), BF16),
-            pltpu.SemaphoreType.DMA((4,)),
-            pltpu.SemaphoreType.DMA((8,)),
-            pltpu.SemaphoreType.DMA((16,)),
         ],
+        compiler_params=grant(24),
         name="scatter_z",
     )(recv, tz)
 
@@ -327,17 +300,9 @@
     return jnp.concatenate([x[:n], x[n:]], 1)
 
 
-def yx_kernel(row_ref, in_hbm, ty_ref, tx_ref, keep_ref, send_ref, in_ref, v_ref, sem):
-    def get(r):
-        at = pl.ds(r * COLS, COLS)
-        return pltpu.make_async_copy(in_hbm.at[at], in_ref.at[at], sem.at[r])
-
-    for r in range(8):
-        get(r).start()
-
+def yx_kernel(row_ref, in_ref, ty_ref, tx_ref, keep_ref, send_ref, v_ref):
     @pl.loop(0, 8, unroll=2)
     def _(r):
-        get(r).wait()
         at = pl.ds(r * COLS, COLS)
         rhs = jnp.concatenate([in_ref[at, :, p].reshape(512, 128) for p in range(2)], 1)
         res = mm(ty_ref[...], rhs)
@@ -363,36 +328,31 @@
 def yx_forward(row, zs, ty, tx):
     smem = pl.BlockSpec(memory_space=pltpu.SMEM)
     vmem = pl.BlockSpec(memory_space=pltpu.VMEM)
-    hbm = pl.BlockSpec(memory_space=pl.ANY)
     return pl.pallas_call(
         yx_kernel,
-        out_shape=(jax.ShapeDtypeStruct((4, 64, 128), BF16),) * 2,
-        in_specs=[smem, hbm, vmem, vmem],
+        out_shape=(pltpu.VMEM((4, 64, 128), BF16),) * 2,
+        in_specs=[smem, vmem, vmem, vmem],
         out_specs=(vmem, vmem),
         scratch_shapes=[
-            pltpu.VMEM((128, 2, 2, 16, 128), BF16),
             pltpu.VMEM((4, 512, 128), BF16),
-            pltpu.SemaphoreType.DMA((8,)),
         ],
+        compiler_params=grant(16),
         name="yx_forward",
     )(row, zs, ty, tx)
 
 
 def mix_kernel(
-    row_ref, own_ref, got_ref, mode_hbm, m1_hbm, m2_hbm, m3_hbm, keep_ref, send_ref, w_ref, sem
+    row_ref, own_ref, got_ref, mode_hbm, m1_ref, m2_ref, m3_ref, keep_ref, send_ref, m0_ref, sem
 ):
     chip = row_ref[0] // 2
     first = row_ref[0] % 2 == 0
-    copies = [
-        pltpu.make_async_copy(src, w_ref.at[d], sem.at[d])
-        for d, src in enumerate((mode_hbm.at[chip], m1_hbm, m2_hbm, m3_hbm))
-    ]
-    for copy in copies:
-        copy.start()
+    copy = pltpu.make_async_copy(mode_hbm.at[chip], m0_ref, sem)
+    copy.start()
     lane = lax.broadcasted_iota(jnp.int32, (16, 128), 1)
 
-    for d in range(4):
-        copies[d].wait()
+    for d, w_ref in ((1, m1_ref), (2, m2_ref), (3, m3_ref), (0, m0_ref)):
+        if d == 0:
+            copy.wait()
         j = (chip + 4 - d) % 4
         spec = choose(first, own_ref[j].astype(F32), got_ref[j].astype(F32))
         swapped = [pltpu.roll(x, 64, 1) for x in spec]
@@ -401,7 +361,7 @@
             a1 = jnp.zeros((16, 128), F32)
             a2 = jnp.zeros((16, 128), F32)
             for c in range(CH):
-                w = w_ref[d, ky, c].astype(F32)
+                w = w_ref[ky, c].astype(F32)
                 at = ky * 8 + c % 8
                 a1 = a1 + spec[c // 8][at : at + 1, :] * w
                 a2 = a2 + swapped[c // 8][at : at + 1, :] * w
@@ -416,25 +376,22 @@
 def mix(row, own, got, modes, parts):
     smem = pl.BlockSpec(memory_space=pltpu.SMEM)
     vmem = pl.BlockSpec(memory_space=pltpu.VMEM)
-    hbm = pl.BlockSpec(memory_space=pl.ANY)
+    hbm = pl.BlockSpec(memory_space=pltpu.HBM)
     return pl.pallas_call(
         mix_kernel,
-        out_shape=(jax.ShapeDtypeStruct((4, 64, 128), BF16),) * 2,
-        in_specs=[smem, vmem, vmem, hbm, hbm, hbm, hbm],
+        out_shape=(pltpu.VMEM((4, 64, 128), BF16),) * 2,
+        in_specs=[smem, vmem, vmem, hbm, vmem, vmem, vmem],
         out_specs=(vmem, vmem),
         scratch_shapes=[
-            pltpu.VMEM((4, 8, CH, CH, 128), BF16),
-            pltpu.SemaphoreType.DMA((4,)),
+            pltpu.VMEM((8, CH, CH, 128), BF16),
+            pltpu.SemaphoreType.DMA,
         ],
+        compiler_params=grant(16),
         name="mix",
     )(row, own, got, modes, *parts)
 
 
-def xy_kernel(row_ref, own_ref, got_ref, ix_ref, iy_ref, out_hbm, u_ref, out_ref, sem):
-    def put(r):
-        at = pl.ds(r * COLS, COLS)
-        return pltpu.make_async_copy(out_ref.at[at], out_hbm.at[at], sem.at[r])
-
+def xy_kernel(row_ref, own_ref, got_ref, ix_ref, iy_ref, out_ref, u_ref):
     @pl.loop(0, 4, unroll=2)
     def _(g):
         pair = choose(row_ref[0] % 2 == 0, own_ref[g].astype(F32), got_ref[g].astype(F32))
@@ -453,26 +410,20 @@
                 at = s * 32 + ri * 16
                 for p in range(2):
                     out_ref[r * COLS + s, ri, p] = res[at : at + 16, p * 128 : p * 128 + 128]
-        put(r).start()
-
-    for r in range(8):
-        put(r).wait()
 
 
 def xy_inverse(row, own, got, ix, iy):
     smem = pl.BlockSpec(memory_space=pltpu.SMEM)
     vmem = pl.BlockSpec(memory_space=pltpu.VMEM)
-    hbm = pl.BlockSpec(memory_space=pl.ANY)
     return pl.pallas_call(
         xy_kernel,
-        out_shape=jax.ShapeDtypeStruct((128, 2, 2, 16, 128), BF16),
+        out_shape=pltpu.VMEM((128, 2, 2, 16, 128), BF16),
         in_specs=[smem, vmem, vmem, vmem, vmem],
-        out_specs=hbm,
+        out_specs=vmem,
         scratch_shapes=[
             pltpu.VMEM((4, 32, 16, 128), BF16),
-            pltpu.VMEM((128, 2, 2, 16, 128), BF16),
-            pltpu.SemaphoreType.DMA((8,)),
         ],
+        compiler_params=grant(16),
         name="xy_inverse",
     )(row, own, got, ix, iy)
 
@@ -505,35 +456,14 @@
 
 
 def final_kernel(
-    ids_ref, yi_hbm, field_hbm, recv_hbm, iz_ref, in_ref, skip_ref, bias_ref, mout_ref, out_hbm,
-    yi_ref, field_ref, tail_ref, out_ref, y_ref, xa_ref, xb_ref, l_ref, w1_ref, w2_ref, b1_ref,
-    yi_sem, field_sem, tail_sem, out_sem, *, ny, unroll
+    ids_ref, yi_ref, field_ref, tail_ref, iz_ref, in_ref, skip_ref, bias_ref, mout_ref, out_ref,
+    y_ref, xa_ref, xb_ref, l_ref, w1_ref, w2_ref, b1_ref, *, ny, unroll
 ):
-    def get_yi(r):
-        at = pl.ds(r * COLS, COLS)
-        return pltpu.make_async_copy(yi_hbm.at[at], yi_ref.at[at], yi_sem.at[r])
-
-    def put_out(i):
-        at = pl.ds(i * 2 * unroll, 2 * unroll)
-        return pltpu.make_async_copy(out_ref.at[at], out_hbm.at[at], out_sem.at[i])
-
-    get_field = pltpu.make_async_copy(field_hbm, field_ref, field_sem)
-    get_tail = pltpu.make_async_copy(recv_hbm.at[:, 32:56], tail_ref, tail_sem)
-
-    @pl.loop(0, 8)
-    def _(r):
-        get_yi(r).start()
-
-    get_field.start()
-    get_tail.start()
     expand_weights(in_ref, skip_ref, mout_ref, w1_ref, w2_ref)
     b1_ref[...] = jnp.concatenate([bias_ref[...]] * 8, 1)
 
     @pl.loop(0, 4)
     def _(kz):
-        get_yi(2 * kz).wait()
-        get_yi(2 * kz + 1).wait()
-
         @pl.loop(0, 16, unroll=4)
         def _(s):
             for ri in range(2):
@@ -566,7 +496,6 @@
         l_ref[pl.ds(i * ny, ny)] = o.reshape(ny, GRID, 128)
 
     steps = 64 // ny
-    get_field.wait()
     stage(0, xa_ref)
 
     @pl.loop(0, steps // 2)
@@ -576,14 +505,12 @@
         stage(jnp.minimum(2 * i + 2, steps - 1), xa_ref)
         layer(2 * i + 1, xb_ref)
 
-    get_tail.wait()
-
     @pl.loop(0, NBLK // unroll)
     def _(i):
         for u in range(unroll):
             d = i * unroll + u
-            weights = tail_ref[d, 0:16, :].astype(F32)
-            heads = tail_ref[d, 16:24, :].astype(F32)
+            weights = tail_ref[d, 32:48, :].astype(F32)
+            heads = tail_ref[d, 48:56, :].astype(F32)
             for j in range(2):
                 head = heads[4 * j : 4 * j + 4]
                 basis = yz_basis(weights[8 * j : 8 * j + 8], head)
@@ -601,28 +528,18 @@
                     )
                     val = jnp.where(vx == float(x), got, val)
                 out_ref[2 * d + j] = val.astype(BF16)
-        put_out(i).start()
-
-    @pl.loop(0, NBLK // unroll)
-    def _(i):
-        put_out(i).wait()
 
 
 def final(ids, yi, field, recv, iz, first, skip, bias, mout):
     smem = pl.BlockSpec(memory_space=pltpu.SMEM)
     vmem = pl.BlockSpec(memory_space=pltpu.VMEM)
-    hbm = pl.BlockSpec(memory_space=pl.ANY)
     ny, unroll = 8, 16
     return pl.pallas_call(
         partial(final_kernel, ny=ny, unroll=unroll),
-        out_shape=jax.ShapeDtypeStruct((NSLOT, 16, NPTS), BF16),
-        in_specs=[smem, hbm, hbm, hbm, vmem, vmem, vmem, vmem, vmem],
-        out_specs=hbm,
+        out_shape=pltpu.VMEM((NSLOT, 16, NPTS), BF16),
+        in_specs=[smem, vmem, vmem, vmem, vmem, vmem, vmem, vmem, vmem],
+        out_specs=vmem,
         scratch_shapes=[
-            pltpu.VMEM((128, 2, 2, 16, 128), BF16),
-            pltpu.VMEM((64, GRID, 128), BF16),
-            pltpu.VMEM((NBLK, 24, NPTS), BF16),
-            pltpu.VMEM((NSLOT, 16, NPTS), BF16),
             pltpu.VMEM((4, 2048, 128), F32),
             pltpu.VMEM((ny * GRID, 256), BF16),
             pltpu.VMEM((ny * GRID, 256), BF16),
@@ -630,11 +547,8 @@
             pltpu.VMEM((256, 512), BF16),
             pltpu.VMEM((512, 128), BF16),
             pltpu.VMEM((1, 512), F32),
-            pltpu.SemaphoreType.DMA((8,)),
-            pltpu.SemaphoreType.DMA,
-            pltpu.SemaphoreType.DMA,
-            pltpu.SemaphoreType.DMA((NBLK // unroll,)),
         ],
+        compiler_params=grant(40),
         name="mlp_gather",
     )(ids, yi, field, recv, iz, first, skip, bias, mout)
 
@@ -654,6 +568,7 @@
         out_shape=jax.ShapeDtypeStruct((CH, NBLK * NPTS), BF16),
         in_specs=[smem, vmem],
         out_specs=vmem,
+        compiler_params=grant(16),
         name="unpack",
     )(slots, vals)
 
@@ -663,7 +578,7 @@
 
 
 def partner(x):
-    return lax.ppermute(x, "row", [(i, i ^ 1) for i in range(ROWS)])
+    return near(lax.ppermute(x, "row", [(i, i ^ 1) for i in range(ROWS)]))
 
 
 def body(
@@ -681,24 +596,25 @@
     tz, ty, tx, ix, iy, iz = tables()
     owner = block_owner.reshape(NBLK)
     row = lax.axis_index("row").astype(jnp.int32)[None]
+    spec_weight = pltpu.with_memory_space_constraint(spec_weight, pltpu.HBM)
     corner = point_corner.reshape(NBLK, NPTS)
     send, slots, *parts = pack(
         row, owner, block_cell, features, point_weights, corner, spec_weight
     )
     parts = [
-        lax.ppermute(part, "row", [(i, (i + 2 * d) % ROWS) for i in range(ROWS)])
+        near(lax.ppermute(part, "row", [(i, (i + 2 * d) % ROWS) for i in range(ROWS)]))
         for d, part in zip((1, 2, 3), parts)
     ]
-    recv = a2a(send, ("row", "col"))
+    recv = near(a2a(send, ("row", "col")))
     field, zs, ids = scatter(recv, tz)
-    zs = a2a(zs.reshape(128, 2, 2, 16, 128), ("row", "col"))
+    zs = near(a2a(zs.reshape(128, 2, 2, 16, 128), ("row", "col")))
     keep, send = yx_forward(row, zs, ty, tx)
     keep, send = mix(row, keep, partner(send), spec_weight, parts)
-    yi = a2a(xy_inverse(row, keep, partner(send), ix, iy), ("row", "col"))
+    yi = near(a2a(xy_inverse(row, keep, partner(send), ix, iy), ("row", "col")))
     vals = final(
         ids, yi, field, recv, iz, mlp_in.T, skip_weight, mlp_bias.reshape(1, HID), mlp_out
     )
-    return unpack(slots, a2a(vals, ("row", "col")))
+    return unpack(slots, near(a2a(vals, ("row", "col"))))
 
 
 def solution(mesh):

time: 210 us -> 204 us (0.971)
  Pallas kernels: 58.1 us -> 45.6 us
  local copies, waits for them, and re-layouts: 2.78 us -> 8.44 us
  waiting for transfers between devices: 34.6 us -> 36.8 us
    pallas_call x6, Pallas kernels: 55.8 us -> 43.9 us  [the longest x1 21.1 us: final(): pl.pallas_call(partial(final_kernel, ny=ny, unroll=unroll), out_shape=plt...]
    unnamed x10 -> x36, local copies, waits for them, and re-layouts: 2.78 us -> 8.44 us
    ppermute x3, waiting for transfers between devices: 9.03 us -> 11.8 us  [body(): lax.ppermute(part, 'row', [(i, (i + 2 * d) % ROWS) for i in range(ROWS)])]
  transfers between devices with their start and end apart: 6 -> 6, of which waited for: 3 -> 4; matrix products, arithmetic and copies ran while one was open for 0% -> 0% of each run, Pallas kernels for 3% -> 2%
where the time goes in v1:
time: 204 us
  blocking collectives  99.2 us (49%)
  Pallas kernels  45.6 us (22%)
  waiting for transfers between devices  36.8 us (18%)
  starting transfers between devices  13.8 us (7%)
  local copies, waits for them, and re-layouts  8.44 us (4%)
    all_to_all x3, blocking collectives, a2a(): return lax.all_to_all(x, axes, split_axis=0, concat_axis=0, tiled=True)  99.2 us
    all_to_all x1, waiting for transfers between devices, a2a(): return lax.all_to_all(x, axes, split_axis=0, concat_axis=0, tiled=True)  24.1 us
    pallas_call x1, Pallas kernels, final(): pl.pallas_call(partial(final_kernel, ny=ny, unroll=unroll), out_shape=plt...  21.1 us
    ppermute x3, waiting for transfers between devices, body(): lax.ppermute(part, 'row', [(i, (i + 2 * d) % ROWS) for i in range(ROWS)])  11.8 us
    pallas_call x1, Pallas kernels, scatter(): pl.pallas_call(partial(scatter_kernel, unroll=16), out_shape=(pltpu.VMEM(...  11 us
    unnamed x36, local copies, waits for them, and re-layouts  8.44 us
    all_to_all x1, starting transfers between devices, a2a(): return lax.all_to_all(x, axes, split_axis=0, concat_axis=0, tiled=True)  6.09 us
    ppermute x3, starting transfers between devices, body(): lax.ppermute(part, 'row', [(i, (i + 2 * d) % ROWS) for i in range(ROWS)])  5.13 us
  transfers between devices with their start and end apart: 6, of which 4 were waited for; matrix products, arithmetic and copies ran while one was open for 0% of the time, Pallas kernels for 2%

profile of v1, /device:TPU:1, one launch (start us, length us, event | category | flops | bytes accessed | tf_op | source)
XLA Modules:
  0.0 204.0 jit_solution(7506245385671179664)
XLA Ops:
  0.0 1.0 copy-done.3
  1.0 0.9 copy-done.4
  4.1 4.3 %pack.1 = (bf16[128,56,128]{2,1,0:T(8,128)(2,1)}, s32[128]{0:T(128)S(1)}, bf16[8,16,16,128]{3,2,1,0:T(8,128)(2,1)}, bf16[8,16,16,128]{3,2,1,0:T(8,128)(2,1)}, bf16[8,16,16,128]{3,2,1,0:T(8,128)(2,1)}) custom-call(s32[1]{0:T(128)} %bitcast.row_ref, s32[128]{0:T(128)S(1)} %bitcast.9, s32[128]{0:T(128)S(1)} %copy-done.16, bf16[16,16384]{1,0:T(8,128)(2,1)S(1)} %copy-done.3, ...), custom_call_target="tpu_custom_call" | custom-call | tf_op jit(solution)/shard_map/pack/pallas_call | solution.py:138
  8.4 38.3 %all_to_all.20.recv_ref.tail_ref = bf16[128,56,128]{2,1,0:T(8,128)(2,1)S(1)} all-to-all(bf16[128,56,128]{2,1,0:T(8,128)(2,1)} %get-tuple-element.18), channel_id=1, replica_groups=mesh['row'=8,'col'=16] {'row','col'}, dimensions={0} | all-to-all | bytes 3670016 | tf_op jit(solution)/shard_map/all_to_all | solution.py:577
  46.7 11.0 %scatter_z.1 = (bf16[64,256,128]{2,1,0:T(8,128)(2,1)S(1)}, bf16[8,16,2,2,16,128]{5,4,3,2,1,0:T(8,128)(2,1)S(1)}, s32[256]{0:T(256)S(1)}) custom-call(bf16[128,56,128]{2,1,0:T(8,128)(2,1)S(1)} %all_to_all.20.recv_ref.tail_ref, bf16[128,256]{1,0:T(8,128)(2,1)S(1)} %copy-done.11), custom_call_target="tpu_custom_call" | custom-call | tf_op jit(solution)/shard_map/scatter_z/pallas_call | solution.py:269
  57.7 1.9 copy-done
  59.6 1.4 copy-done.2
  61.0 6.1 %all-to-all-start.1 = ((bf16[128,2,2,16,128]{4,3,2,1,0:T(8,128)(2,1)}), bf16[128,2,2,16,128]{4,3,2,1,0:T(8,128)(2,1)}, u32[]{:S(2)}, u32[]{:S(2)}) async-start(bf16[128,2,2,16,128]{4,3,2,1,0:T(8,128)(2,1)} %bitcast.6), calls=%async_computation.1 | async-start | bytes 4194304 | tf_op jit(solution)/shard_map/all_to_all | solution.py:577
  67.1 1.5 collective-permute-start.1
  68.6 2.5 %collective-permute-start.2 = (bf16[8,16,16,128]{3,2,1,0:T(8,128)(2,1)}, bf16[8,16,16,128]{3,2,1,0:T(8,128)(2,1)S(1)}, u32[]{:S(2)}, u32[]{:S(2)}) collective-permute-start(bf16[8,16,16,128]{3,2,1,0:T(8,128)(2,1)} %get-tuple-element.24), channel_id=1, source_target_pairs={{0,64},{16,80},{32,96},{48,112},{64,0},{80,16},{96,32},{112,48},{1... | collective-permute-start | bytes 1572872 | tf_op jit(solution)/shard_map/ppermute | solution.py:605
  71.1 1.1 collective-permute-start.3
  72.3 24.1 %all-to-all-done.1.in_ref = bf16[128,2,2,16,128]{4,3,2,1,0:T(8,128)(2,1)} async-done(((bf16[128,2,2,16,128]{4,3,2,1,0:T(8,128)(2,1)}), bf16[128,2,2,16,128]{4,3,2,1,0:T(8,128)(2,1)}, u32[]{:S(2)}, u32[]{:S(2)}) %all-to-all-start.1) | async-done | bytes 2097184 | tf_op jit(solution)/shard_map/all_to_all | solution.py:577
  96.3 0.9 copy-done.6
  97.2 4.0 %yx_forward.1 = (bf16[4,64,128]{2,1,0:T(8,128)(2,1)S(1)}, bf16[4,64,128]{2,1,0:T(8,128)(2,1)S(1)}) custom-call(s32[1]{0:T(128)} %bitcast.row_ref, bf16[128,2,2,16,128]{4,3,2,1,0:T(8,128)(2,1)} %all-to-all-done.1.in_ref, bf16[128,512]{1,0:T(8,128)(2,1)S(1)} %copy-done.6, bf16[128,512]{1,0:T(8,128)(2,1)S(1)} %copy-done.5), custom_call_target="tpu_custom_call" | custom-call | tf_op jit(solution)/shard_map/yx_forward/pallas_call | solution.py:331
  101.3 1.5 collective-permute-start
  103.5 11.2 %collective-permute-done.2.m2_ref = bf16[8,16,16,128]{3,2,1,0:T(8,128)(2,1)S(1)} collective-permute-done((bf16[8,16,16,128]{3,2,1,0:T(8,128)(2,1)}, bf16[8,16,16,128]{3,2,1,0:T(8,128)(2,1)S(1)}, u32[]{:S(2)}, u32[]{:S(2)}) %collective-permute-start.2) | collective-permute-done | bytes 524320 | tf_op jit(solution)/shard_map/ppermute | solution.py:605
  114.6 1.4 mix.1
  116.0 1.0 collective-permute-start.4
  117.1 0.9 collective-permute-done.4.got_ref
  118.0 2.2 %xy_inverse.1 = bf16[128,2,2,16,128]{4,3,2,1,0:T(8,128)(2,1)S(1)} custom-call(s32[1]{0:T(128)} %bitcast.row_ref, bf16[4,64,128]{2,1,0:T(8,128)(2,1)S(1)} %get-tuple-element.26.own_ref, bf16[4,64,128]{2,1,0:T(8,128)(2,1)S(1)} %collective-permute-done.4.got_ref, bf16[512,128]{1,0:T(8,128)(2,1)S(1)} %copy-done.8, bf16[512,128]{1,0:T(8,128)(2,1)S(1)} %copy-done.7), custom_call_target="tpu_custom_call" | custom-call | tf_op jit(solution)/shard_map/xy_inverse/pallas_call | solution.py:418
  120.2 37.0 %all_to_all.21.yi_ref = bf16[128,2,2,16,128]{4,3,2,1,0:T(8,128)(2,1)S(1)} all-to-all(bf16[128,2,2,16,128]{4,3,2,1,0:T(8,128)(2,1)S(1)} %xy_inverse.1), channel_id=1, replica_groups=mesh['row'=8,'col'=16] {'row','col'}, dimensions={0} | all-to-all | bytes 4194304 | tf_op jit(solution)/shard_map/all_to_all | solution.py:577
  157.3 21.1 %mlp_gather.1 = bf16[256,16,128]{2,1,0:T(8,128)(2,1)S(1)} custom-call(s32[256]{0:T(256)S(1)} %get-tuple-element.19.ids_ref, bf16[128,2,2,16,128]{4,3,2,1,0:T(8,128)(2,1)S(1)} %all_to_all.21.yi_ref, bf16[64,256,128]{2,1,0:T(8,128)(2,1)S(1)} %copy-done.1, bf16[128,56,128]{2,1,0:T(8,128)(2,1)S(1)} %all_to_all.20.recv_ref.tail_ref, ...), custom_call_target="tpu_custom_call" | custom-call | tf_op jit(solution)/shard_map/mlp_gather/pallas_call | solution.py:537
  178.4 23.9 %all_to_all.22.in_ref = bf16[256,16,128]{2,1,0:T(8,128)(2,1)S(1)} all-to-all(bf16[256,16,128]{2,1,0:T(8,128)(2,1)S(1)} %mlp_gather.1), channel_id=1, replica_groups=mesh['row'=8,'col'=16] {'row','col'}, dimensions={0} | all-to-all | bytes 2097152 | tf_op jit(solution)/shard_map/all_to_all | solution.py:577
  202.3 1.7 unpack.1
  (34 shorter events, 2.9 us)
Async XLA Ops:
  0.0 1.0 copy-start.3
  1.0 0.9 copy-start.4
  2.0 0.8 copy-start.10
  2.8 0.7 copy-start.15
  3.5 0.7 copy-start.16
  8.4 38.3 %copy-start.11 = (bf16[128,256]{1,0:T(8,128)(2,1)S(1)}, bf16[128,256]{1,0:T(8,128)(2,1)}, u32[]{:S(2)}) copy-start(bf16[128,256]{1,0:T(8,128)(2,1)} %constant.25.tz_ref) | copy-start | bytes 196612
  57.7 1.9 copy-start
  59.6 1.4 copy-start.2
  61.0 35.3 %copy-start.5 = (bf16[128,512]{1,0:T(8,128)(2,1)S(1)}, bf16[128,512]{1,0:T(8,128)(2,1)}, u32[]{:S(2)}) copy-start(bf16[128,512]{1,0:T(8,128)(2,1)} %constant.27.tx_ref) | copy-start | bytes 393220
  61.0 35.3 %all-to-all-start.1 = ((bf16[128,2,2,16,128]{4,3,2,1,0:T(8,128)(2,1)}), bf16[128,2,2,16,128]{4,3,2,1,0:T(8,128)(2,1)}, u32[]{:S(2)}, u32[]{:S(2)}) async-start(bf16[128,2,2,16,128]{4,3,2,1,0:T(8,128)(2,1)} %bitcast.6), calls=%async_computation.1 | async-start | bytes 4194304 | tf_op jit(solution)/shard_map/all_to_all | solution.py:577
  67.1 36.3 %collective-permute-start.1 = (bf16[8,16,16,128]{3,2,1,0:T(8,128)(2,1)}, bf16[8,16,16,128]{3,2,1,0:T(8,128)(2,1)S(1)}, u32[]{:S(2)}, u32[]{:S(2)}) collective-permute-start(bf16[8,16,16,128]{3,2,1,0:T(8,128)(2,1)} %get-tuple-element.23), channel_id=1, source_target_pairs={{0,32},{16,48},{32,64},{48,80},{64,96},{80,112},{96,0},{112,16},{1... | collective-permute-start | bytes 1572872 | tf_op jit(solution)/shard_map/ppermute | solution.py:605
  68.6 46.0 %collective-permute-start.2 = (bf16[8,16,16,128]{3,2,1,0:T(8,128)(2,1)}, bf16[8,16,16,128]{3,2,1,0:T(8,128)(2,1)S(1)}, u32[]{:S(2)}, u32[]{:S(2)}) collective-permute-start(bf16[8,16,16,128]{3,2,1,0:T(8,128)(2,1)} %get-tuple-element.24), channel_id=1, source_target_pairs={{0,64},{16,80},{32,96},{48,112},{64,0},{80,16},{96,32},{112,48},{1... | collective-permute-start | bytes 1572872 | tf_op jit(solution)/shard_map/ppermute | solution.py:605
  71.1 43.5 %collective-permute-start.3 = (bf16[8,16,16,128]{3,2,1,0:T(8,128)(2,1)}, bf16[8,16,16,128]{3,2,1,0:T(8,128)(2,1)S(1)}, u32[]{:S(2)}, u32[]{:S(2)}) collective-permute-start(bf16[8,16,16,128]{3,2,1,0:T(8,128)(2,1)} %get-tuple-element.25), channel_id=1, source_target_pairs={{0,96},{16,112},{32,0},{48,16},{64,32},{80,48},{96,64},{112,80},{1... | collective-permute-start | bytes 1572872 | tf_op jit(solution)/shard_map/ppermute | solution.py:605
  96.3 0.9 copy-start.6
  101.3 16.7 %copy-start.7 = (bf16[512,128]{1,0:T(8,128)(2,1)S(1)}, bf16[512,128]{1,0:T(8,128)(2,1)}, u32[]{:S(2)}) copy-start(bf16[512,128]{1,0:T(8,128)(2,1)} %constant.29.iy_ref) | copy-start | bytes 393220
  101.3 16.7 %copy-start.8 = (bf16[512,128]{1,0:T(8,128)(2,1)S(1)}, bf16[512,128]{1,0:T(8,128)(2,1)}, u32[]{:S(2)}) copy-start(bf16[512,128]{1,0:T(8,128)(2,1)} %constant.28.ix_ref) | copy-start | bytes 393220
  101.3 13.3 %collective-permute-start = (bf16[4,64,128]{2,1,0:T(8,128)(2,1)S(1)}, bf16[4,64,128]{2,1,0:T(8,128)(2,1)S(1)}, u32[]{:S(2)}, u32[]{:S(2)}) collective-permute-start(bf16[4,64,128]{2,1,0:T(8,128)(2,1)S(1)} %get-tuple-element.22), channel_id=1, source_target_pairs={{0,16},{16,0},{32,48},{48,32},{64,80},{80,64},{96,112},{112,96},{1... | collective-permute-start | bytes 196616 | tf_op jit(solution)/shard_map/ppermute | solution.py:581
  116.0 1.9 collective-permute-start.4
  118.0 39.3 %copy-start.9 = (bf16[256,128]{1,0:T(8,128)(2,1)S(1)}, bf16[256,128]{1,0:T(8,128)(2,1)}, u32[]{:S(2)}) copy-start(bf16[256,128]{1,0:T(8,128)(2,1)} %constant.30.iz_ref) | copy-start | bytes 196612
  118.0 39.3 %copy-start.13 = (bf16[16,16]{1,0:T(8,128)(2,1)S(1)}, bf16[16,16]{1,0:T(8,128)(2,1)}, u32[]{:S(2)}) copy-start(bf16[16,16]{1,0:T(8,128)(2,1)} %skip_ref.1) | copy-start | bytes 1540
  118.0 39.3 %copy-start.14 = (bf16[16,64]{1,0:T(8,128)(2,1)S(1)}, bf16[16,64]{1,0:T(8,128)(2,1)}, u32[]{:S(2)}) copy-start(bf16[16,64]{1,0:T(8,128)(2,1)} %mout_ref.1) | copy-start | bytes 6148
  120.2 37.1 %copy-start.1 = (bf16[64,256,128]{2,1,0:T(8,128)(2,1)S(1)}, bf16[64,256,128]{2,1,0:T(8,128)(2,1)}, u32[]{:S(2)}) copy-start(bf16[64,256,128]{2,1,0:T(8,128)(2,1)} %copy-done) | copy-start | bytes 12582916
  120.2 37.1 %copy-start.12 = (bf16[64,16]{0,1:T(8,128)(2,1)S(1)}, bf16[64,16]{0,1:T(8,128)(2,1)}, u32[]{:S(2)}) copy-start(bf16[64,16]{0,1:T(8,128)(2,1)} %param.23) | copy-start | bytes 6148
  120.2 37.1 %copy-start.17 = (f32[64]{0:T(128)S(1)}, f32[64]{0:T(128)}, u32[]{:S(2)}) copy-start(f32[64]{0:T(128)} %param.24) | copy-start | bytes 772
